TPU v7x, 32 devices: a whole 2x2x4 slice. The times are simulated.
32 devices in a mesh: row: 4 (over y, x), col: 4 (over z), depth: 2 (over core).
Axes of the slice: x: 2, y: 2, z: 4, core: 2. Of those that a mesh axis runs over, the one named last changes fastest.
Arguments:
- a_blocks: bfloat16 [32, 32, 2, 128, 128], P(('row', 'col', 'depth')), may hold values from -1.25 to 1.25
- a_columns: int32 [32, 32, 2], P(('row', 'col', 'depth')), may hold values from 0 to 319, as said below
- a_live: int32 [32, 32, 2], P(('row', 'col', 'depth')), may hold values from 0 to 1
- atom_rows: int32 [32], P(('row', 'col', 'depth')), may hold values from 0 to 31, as said below
- b_blocks: bfloat16 [320, 4, 6, 128, 128], P(('row', 'depth'), 'col'), may hold values from -1.25 to 1.25
- b_columns: int32 [320, 4, 6], P(('row', 'depth'), 'col'), may hold values from 0 to 319, as said below
- b_live: int32 [320, 4, 6], P(('row', 'depth'), 'col'), may hold values from 0 to 1, as said below
- c_columns: int32 [32, 4, 8], P('row', 'col'), may hold values from 0 to 319, as said below
- c_live: int32 [32, 4, 8], P('row', 'col'), may hold values from 0 to 1
Outputs:
- product: bfloat16 [32, 4, 8, 128, 128], P('row', 'col', 'depth')
Inputs may be any that keep to these rules, and one draw needn't show every extreme that they name: `a_columns`: columns of one block row and group g are distinct and lie in g * 10 to (g + 1) * 10 - 1, also in empty slots. `atom_rows`: A permutation that maps every aligned run of 8 atom-order rows onto the same run of block rows. `b_columns`: columns of one block row and panel c are distinct and lie in c * 80 to (c + 1) * 80 - 1, also in empty slots. `b_live`: live slots of block row k hold columns within 16 of k, counted round. `c_columns`: columns of one block row and panel c are distinct and lie in c * 80 to (c + 1) * 80 - 1.
All inputs are finite; a program needn't handle non-finite values.
Results may differ from a plain program's by a relative error of at most 0.0043.
Values may be sent and summed in bfloat16 or wider, within the bound.
A program may use at most 320 MiB of HBM per device.

v0:
```python
import jax
import jax.numpy as jnp
from jax import lax
from jax.sharding import PartitionSpec as P

GW = 10


def shifted(value, axis, by):
    length = lax.axis_size(axis)
    return lax.ppermute(value, axis, [(i, (i + by) % length) for i in range(length)])


def on_device(
    a_blocks, a_columns, a_live, atom_rows, b_blocks, b_columns, b_live, c_columns, c_live
):
    row_count = lax.axis_size("row")
    col_count = lax.axis_size("col")
    depth_count = lax.axis_size("depth")
    turn_count = min(row_count, col_count)
    row_index = lax.axis_index("row")
    own_rows, group_count, slot_count = a_columns.shape
    block_edge = a_blocks.shape[-1]
    stripe = b_blocks.shape[0]
    per_stripe = stripe // GW
    stripes_piece = row_count // turn_count
    piece_groups = stripes_piece * per_stripe
    dest_col = jnp.arange(col_count, dtype=jnp.int32)[:, None, None]
    dest_layer = jnp.arange(depth_count, dtype=jnp.int32)[None, :, None]
    within = jnp.arange(piece_groups, dtype=jnp.int32)[None, None, :]
    piece_of = (dest_col + row_index) % turn_count
    stripe_ids = (piece_of * stripes_piece + within // per_stripe) * depth_count + dest_layer
    group_ids = (stripe_ids * per_stripe + within % per_stripe).reshape(-1)
    lead_shape = (col_count, depth_count, own_rows, piece_groups, slot_count)
    send_blocks = jnp.moveaxis(jnp.take(a_blocks, group_ids, axis=1), 1, 0).reshape(
        lead_shape + (block_edge, block_edge)
    )
    send_columns = jnp.moveaxis(jnp.take(a_columns, group_ids, axis=1), 1, 0).reshape(lead_shape)
    outgoing_live_flags = jnp.moveaxis(jnp.take(a_live, group_ids, axis=1), 1, 0).reshape(
        lead_shape
    )
    send_rows = jnp.broadcast_to(atom_rows[None, None, :], (col_count, depth_count, own_rows))
    pair_count = col_count * depth_count
    got_blocks, got_columns, got_live, got_rows = (
        lax.all_to_all(
            send_blocks.reshape((pair_count,) + lead_shape[2:] + (block_edge, block_edge)),
            ("col", "depth"),
            split_axis=0,
            concat_axis=0,
            tiled=True,
        ),
        lax.all_to_all(
            send_columns.reshape((pair_count,) + lead_shape[2:]),
            ("col", "depth"),
            split_axis=0,
            concat_axis=0,
            tiled=True,
        ),
        lax.all_to_all(
            outgoing_live_flags.reshape((pair_count,) + lead_shape[2:]),
            ("col", "depth"),
            split_axis=0,
            concat_axis=0,
            tiled=True,
        ),
        lax.all_to_all(
            send_rows.reshape(pair_count, own_rows),
            ("col", "depth"),
            split_axis=0,
            concat_axis=0,
            tiled=True,
        ),
    )
    panel_rows = got_rows.reshape(-1)
    panel_count = panel_rows.shape[0]
    local_rows = panel_rows - row_index * panel_count
    positions = jnp.arange(panel_count, dtype=jnp.int32)
    matched_pairs = local_rows[None, :] == positions[:, None]
    source_of = jnp.sum(jnp.where(matched_pairs, positions[None, :], 0), axis=1)
    block_tiles = got_blocks.reshape(panel_count, -1, block_edge, block_edge)
    columns = got_columns.reshape(panel_count, -1)
    live_flags = got_live.reshape(panel_count, -1)
    layer_blocks, layer_columns, layer_active_flags = (
        lax.all_gather(b_blocks, "row", axis=0, tiled=True),
        lax.all_gather(b_columns, "row", axis=0, tiled=True),
        lax.all_gather(b_live, "row", axis=0, tiled=True),
    )
    list_width = b_columns.shape[2]
    layer_blocks = layer_blocks.reshape(-1, list_width, block_edge, block_edge)
    layer_columns = layer_columns.reshape(-1, list_width)
    layer_active_flags = layer_active_flags.reshape(-1, list_width)
    wanted = jnp.take(c_columns[:, 0, :], local_rows, axis=0)
    partial_value = jnp.zeros((panel_count, wanted.shape[1], block_edge, block_edge), jnp.float32)
    for turn_index in range(turn_count):
        layer_row_index = columns // stripe // depth_count * stripe + columns % stripe
        found_columns = jnp.take(layer_columns, layer_row_index, axis=0)
        found_live = jnp.take(layer_active_flags, layer_row_index, axis=0)
        usable = (found_live > 0) & (live_flags[:, :, None] > 0)
        hits = (found_columns[:, None, :, :] == wanted[:, :, None, None]) & usable[:, None, :, :]
        mapping = hits.astype(jnp.float32)
        selected_entries = jnp.take(layer_blocks, layer_row_index, axis=0)
        block_products = jnp.einsum(
            "rvab,rvsbe->rvsae", block_tiles, selected_entries, preferred_element_type=jnp.float32
        )
        partial_value = partial_value + jnp.einsum(
            "ruvs,rvsae->ruae", mapping, block_products, precision=lax.Precision.HIGHEST
        )
        if turn_index + 1 < turn_count:
            block_tiles, columns, live_flags = shifted(
                (block_tiles, columns, live_flags), "col", -1
            )
    share_count = wanted.shape[1] // depth_count
    depth_index = lax.axis_index("depth")
    summed = lax.psum(partial_value.astype(jnp.bfloat16), "depth").astype(jnp.float32)
    my_share = lax.dynamic_slice_in_dim(summed, depth_index * share_count, share_count, 1)
    my_share = jnp.take(my_share, source_of, axis=0)
    keep_flags = lax.dynamic_slice_in_dim(
        c_live[:, 0, :], depth_index * share_count, share_count, 1
    )
    result = jnp.where(keep_flags[..., None, None] > 0, my_share, jnp.float32(0.0)).astype(
        jnp.bfloat16
    )
    return result[:, None]


def solution(mesh):
    placed = (
        P(("row", "col", "depth"), None, None, None, None),
        P(("row", "col", "depth"), None, None),
        P(("row", "col", "depth"), None, None),
        P(("row", "col", "depth")),
        P(("row", "depth"), "col", None, None, None),
        P(("row", "depth"), "col", None),
        P(("row", "depth"), "col", None),
        P("row", "col", None),
        P("row", "col", None),
    )
    return jax.shard_map(
        on_device,
        mesh=mesh,
        in_specs=placed,
        out_specs=P("row", "col", "depth", None, None),
        check_vma=False,
    )
```

profile of v0, /device:TPU:31, one launch (start us, length us, event | category | flops | bytes accessed | tf_op | source)
XLA Modules:
  0.0 683.6 jit_solution(8725497915445718610)
XLA Ops:
  8.5 5.4 all-to-all-start
  16.3 4.1 broadcast_select_fusion
  20.4 5.1 all-to-all-start.3
  28.7 6.9 %all_gather.10 = s32[160,1,6]{2,0,1:T(8,128)S(1)} all-gather(s32[40,1,6]{2,0,1:T(8,128)S(1)} %copy.229), channel_id=1, replica_groups=mesh['row'=4,'col'=4,'depth'=2] {'row'}, dimensions={0}, use_global_device_ids=true | all-gather | bytes 4800 | tf_op jit(solution)/shard_map/all_gather | solution.py:86
  35.5 7.8 %all_gather.9 = s32[160,1,6]{2,0,1:T(8,128)S(1)} all-gather(s32[40,1,6]{2,0,1:T(8,128)S(1)} %copy.225), channel_id=1, replica_groups=mesh['row'=4,'col'=4,'depth'=2] {'row'}, dimensions={0}, use_global_device_ids=true | all-gather | bytes 4800 | tf_op jit(solution)/shard_map/all_gather | solution.py:85
  43.6 28.4 %all-to-all-done.3 = bf16[8,1,4,2,128,128]{5,4,3,2,1,0:T(8,128)(2,1)} async-done(((bf16[8,1,4,2,128,128]{5,4,3,2,1,0:T(8,128)(2,1)}), bf16[8,1,4,2,128,128]{5,4,3,2,1,0:T(8,128)(2,1)}, u32[]{:S(2)}, u32[]{:S(2)}) %all-to-all-start.3) | async-done | bytes 2097184 | tf_op jit(solution)/shard_map/all_to_all | solution.py:45
  72.0 5.9 all-to-all-start.1
  80.3 6.5 all-to-all-start.2
  87.5 40.4 %all-to-all-done.2 = s32[8,1,4,2]{2,3,1,0:T(2,128)S(1)} async-done(((s32[8,1,4,2]{2,3,1,0:T(2,128)}), s32[8,1,4,2]{2,3,1,0:T(2,128)S(1)}, u32[]{:S(2)}, u32[]{:S(2)}) %all-to-all-start.2) | async-done | bytes 288 | tf_op jit(solution)/shard_map/all_to_all | solution.py:59
  139.3 42.3 %collective-permute-done.4 = s32[8,8]{0,1:T(8,128)S(1)} collective-permute-done((s32[8,8]{0,1:T(8,128)S(1)}, s32[8,8]{0,1:T(8,128)S(1)}, u32[]{:S(2)}, u32[]{:S(2)}) %collective-permute-start.4) | collective-permute-done | bytes 288 | tf_op jit(solution)/shard_map/ppermute | solution.py:11
  189.7 100.7 %all-gather.2.cloned.1.call-done = bf16[160,1,6,128,128]{4,3,2,1,0:T(8,128)(2,1)} async-done(((bf16[40,1,6,128,128]{4,3,2,1,0:T(8,128)(2,1)}), bf16[160,1,6,128,128]{4,3,2,1,0:T(8,128)(2,1)}) %all-gather.2.cloned.1.call-update) | async-done | bytes 31457296 | tf_op jit(solution)/shard_map/all_gather | solution.py:84
  290.3 17.2 %gather_fusion.7 = bf16[64,6,128,128]{3,2,1,0:T(8,128)(2,1)} fusion(bf16[160,6,128,128]{3,2,1,0:T(8,128)(2,1)} %bitcast.147, s32[1024]{0:T(1024)S(1)} %pad_clamp_fusion.6), kind=kCustom, calls=%fused_computation.2.clone | custom fusion | bytes 25166080 | tf_op jit(solution)/shard_map/jit(_take)/gather | solution.py:101
  307.5 17.2 %gather_fusion.10 = bf16[64,6,128,128]{3,2,1,0:T(8,128)(2,1)} fusion(bf16[160,6,128,128]{3,2,1,0:T(8,128)(2,1)} %bitcast.148, s32[1024]{0:T(1024)S(1)} %pad_clamp_fusion.3), kind=kCustom, calls=%fused_computation.11.clone | custom fusion | bytes 25166080 | tf_op jit(solution)/shard_map/jit(_take)/gather | solution.py:101
  324.7 16.6 %copy.239 = bf16[8,8,6,128,128]{3,4,2,1,0:T(8,128)(2,1)} copy(bf16[8,8,6,128,128]{4,3,2,1,0:T(8,128)(2,1)} %bitcast.153) | data formatting | bytes 25165824 | tf_op jit(solution)/shard_map/jit(_take)/gather | solution.py:101
  341.3 16.7 %copy.250 = bf16[8,8,6,128,128]{3,4,2,1,0:T(8,128)(2,1)} copy(bf16[8,8,6,128,128]{4,3,2,1,0:T(8,128)(2,1)} %bitcast.154) | data formatting | bytes 25165824 | tf_op jit(solution)/shard_map/jit(_take)/gather | solution.py:101
  358.0 13.6 %fusion.12 = f32[8,8,6,128,128]{3,4,2,1,0:T(8,128)} fusion(bf16[8,8,128,128,1]{3,2,4,1,0:T(8,128)(2,1)} %bitcast.24, bf16[8,8,6,128,128]{3,4,2,1,0:T(8,128)(2,1)} %copy.239, pred[8,8]{1,0:T(8,128)(4,1)S(1)} %copy.224), kind=kOutput, calls=%fused_computation.29 | convolution fusion | flops 1616904192 | bytes 39845952 | tf_op jit(solution)/shard_map/rvab,rvsbe->rvsae/dot_general | solution.py:102
  371.6 13.7 %fusion.15 = f32[8,8,6,128,128]{3,4,2,1,0:T(8,128)} fusion(bf16[8,8,6,128,128]{3,4,2,1,0:T(8,128)(2,1)} %copy.250, pred[8,8]{1,0:T(8,128)(4,1)S(1)} %copy.241, bf16[8,8,128,128]{3,2,1,0:T(8,128)(2,1)} %collective-permute-done.2), kind=kOutput, calls=%fused_computation.30 | convolution fusion | flops 1616904192 | bytes 39845952 | tf_op jit(solution)/shard_map/rvab,rvsbe->rvsae/dot_general | solution.py:102
  385.3 17.2 %gather_fusion.13 = bf16[64,6,128,128]{3,2,1,0:T(8,128)(2,1)} fusion(bf16[160,6,128,128]{3,2,1,0:T(8,128)(2,1)} %bitcast.149, s32[1024]{0:T(1024)S(1)} %pad_clamp_fusion.2), kind=kCustom, calls=%fused_computation.12.clone | custom fusion | bytes 25166080 | tf_op jit(solution)/shard_map/jit(_take)/gather | solution.py:101
  402.5 17.1 %gather_fusion.16 = bf16[64,6,128,128]{3,2,1,0:T(8,128)(2,1)} fusion(bf16[160,6,128,128]{3,2,1,0:T(8,128)(2,1)} %bitcast.150, s32[1024]{0:T(1024)S(1)} %pad_clamp_fusion.1), kind=kCustom, calls=%fused_computation.13.clone | custom fusion | bytes 25166080 | tf_op jit(solution)/shard_map/jit(_take)/gather | solution.py:101
  419.6 24.8 %copy.240 = f32[8,8,6,128,128]{4,1,2,3,0:T(8,128)} copy(f32[8,8,6,128,128]{3,4,2,1,0:T(8,128)} %fusion.12) | data formatting | bytes 50331648 | tf_op jit(solution)/shard_map/rvab,rvsbe->rvsae/transpose | solution.py:102
  444.4 24.9 %copy.251 = f32[8,8,6,128,128]{4,1,2,3,0:T(8,128)} copy(f32[8,8,6,128,128]{3,4,2,1,0:T(8,128)} %fusion.15) | data formatting | bytes 50331648 | tf_op jit(solution)/shard_map/rvab,rvsbe->rvsae/transpose | solution.py:102
  469.3 16.6 %copy.272 = bf16[8,8,6,128,128]{3,4,2,1,0:T(8,128)(2,1)} copy(bf16[8,8,6,128,128]{4,3,2,1,0:T(8,128)(2,1)} %bitcast.152) | data formatting | bytes 25165824 | tf_op jit(solution)/shard_map/jit(_take)/gather | solution.py:101
  485.9 16.7 %copy.261 = bf16[8,8,6,128,128]{3,4,2,1,0:T(8,128)(2,1)} copy(bf16[8,8,6,128,128]{4,3,2,1,0:T(8,128)(2,1)} %bitcast.151) | data formatting | bytes 25165824 | tf_op jit(solution)/shard_map/jit(_take)/gather | solution.py:101
  502.6 13.8 %fusion.18 = f32[8,8,6,128,128]{3,4,2,1,0:T(8,128)} fusion(bf16[8,8,6,128,128]{3,4,2,1,0:T(8,128)(2,1)} %copy.261, pred[8,8]{1,0:T(8,128)(4,1)S(1)} %copy.252, bf16[8,8,128,128]{3,2,1,0:T(8,128)(2,1)} %collective-permute-done.5), kind=kOutput, calls=%fused_computation.31 | convolution fusion | flops 1616904192 | bytes 39845952 | tf_op jit(solution)/shard_map/rvab,rvsbe->rvsae/dot_general | solution.py:102
  516.4 24.8 %copy.262 = f32[8,8,6,128,128]{4,1,2,3,0:T(8,128)} copy(f32[8,8,6,128,128]{3,4,2,1,0:T(8,128)} %fusion.18) | data formatting | bytes 50331648 | tf_op jit(solution)/shard_map/rvab,rvsbe->rvsae/transpose | solution.py:102
  541.2 12.9 %fusion.21 = f32[8,8,6,128,128]{3,4,2,1,0:T(8,128)} fusion(bf16[8,8,6,128,128]{3,4,2,1,0:T(8,128)(2,1)} %copy.272, pred[8,8]{1,0:T(8,128)(4,1)S(1)} %copy.263, bf16[8,8,128,128]{3,2,1,0:T(8,128)(2,1)S(1)} %collective-permute-done.8), kind=kOutput, calls=%fused_computation.32 | convolution fusion | flops 1616904192 | bytes 39845952 | tf_op jit(solution)/shard_map/rvab,rvsbe->rvsae/dot_general | solution.py:102
  554.1 24.9 %copy.273 = f32[8,8,6,128,128]{4,1,2,3,0:T(8,128)} copy(f32[8,8,6,128,128]{3,4,2,1,0:T(8,128)} %fusion.21) | data formatting | bytes 50331648 | tf_op jit(solution)/shard_map/rvab,rvsbe->rvsae/transpose | solution.py:102
  579.0 15.6 %fusion.39 = f32[8,8,128,128,1]{3,1,4,2,0:T(8,128)} fusion(f32[8,8,6,128,128]{4,1,2,3,0:T(8,128)} %copy.240, s32[8,8]{1,0:T(8,128)S(1)} %copy-done.7, s32[8,8,6]{1,2,0:T(8,128)S(1)} %copy-done.3, pred[8,8,6]{1,2,0:T(8,128)(4,1)S(1)} %copy-done.8), kind=kOutput, calls=%fused_computation.54 | convolution fusion | flops 603985920 | bytes 29362304 | tf_op jit(solution)/shard_map/ruvs,rvsae->ruae/dot_general | solution.py:105
  594.7 15.6 %fusion.37 = f32[8,8,128,128,1]{3,1,4,2,0:T(8,128)} fusion(f32[8,8,6,128,128]{4,1,2,3,0:T(8,128)} %copy.251, s32[8,8,6]{1,2,0:T(8,128)S(1)} %copy-done.4, s32[8,8]{1,0:T(8,128)S(1)} %copy-done.7, pred[8,8,6]{1,2,0:T(8,128)(4,1)S(1)} %copy-done.9), kind=kOutput, calls=%fused_computation.52 | convolution fusion | flops 603985920 | bytes 29362304 | tf_op jit(solution)/shard_map/ruvs,rvsae->ruae/dot_general | solution.py:105
  610.3 15.9 %fusion.35 = f32[8,8,128,128,1]{3,1,4,2,0:T(8,128)} fusion(f32[8,8,6,128,128]{4,1,2,3,0:T(8,128)} %copy.262, s32[8,8,6]{1,2,0:T(8,128)S(1)} %copy-done.5, s32[8,8]{1,0:T(8,128)S(1)} %copy-done.7, pred[8,8,6]{1,2,0:T(8,128)(4,1)S(1)} %copy-done.10), kind=kOutput, calls=%fused_computation.50 | convolution fusion | flops 603985920 | bytes 29362304 | tf_op jit(solution)/shard_map/ruvs,rvsae->ruae/dot_general | solution.py:105
  626.2 19.4 %fusion.28 = bf16[8,8,128,128]{3,1,2,0:T(8,128)(2,1)} fusion(f32[8,8,128,128,1]{3,1,4,2,0:T(8,128)} %fusion.35, f32[8,8,128,128,1]{3,1,4,2,0:T(8,128)} %fusion.37, f32[8,8,128,128,1]{3,1,4,2,0:T(8,128)} %fusion.39, f32[8,8,6,128,128]{4,1,2,3,0:T(8,128)} %copy.273, s32[8,8,6]{1,2,0:T(8,128)S(1)} %copy-done.6, s32[8,8]{1,0:T(8,128)S(1)} %copy-done.7, ...), kind=kOutput, calls=%fused_computation.38 | convolution fusion | flops 608180224 | bytes 39848064 | tf_op jit(solution)/shard_map/ruvs,rvsae->ruae/dot_general | solution.py:105
  646.0 22.7 %all-reduce.2.cloned.1.call-done = bf16[8,8,128,128]{3,1,2,0:T(8,128)(2,1)} async-done(((bf16[8,8,128,128]{3,1,2,0:T(8,128)(2,1)}), bf16[8,8,128,128]{3,1,2,0:T(8,128)(2,1)}) %all-reduce.2.cloned.1.call-update) | async-done | bytes 2097168 | tf_op jit(solution)/shard_map/psum | solution.py:114
  (160 shorter events, 37.5 us)
Async XLA Ops:
  6.5 19.1 %copy-start.15 = (s32[1,32,2]{1,2,0:T(2,128)S(1)}, s32[1,32,2]{1,2,0:T(2,128)}, u32[]{:S(2)}) copy-start(s32[1,32,2]{1,2,0:T(2,128)} %param.16) | copy-start | bytes 772
  6.5 19.8 %copy-start.16 = (s32[1,32,2]{1,2,0:T(2,128)S(1)}, s32[1,32,2]{1,2,0:T(2,128)}, u32[]{:S(2)}) copy-start(s32[1,32,2]{1,2,0:T(2,128)} %param.17) | copy-start | bytes 772
  6.5 22.0 %copy-start.13 = (s32[40,1,6]{0,1,2:T(1,128)S(1)}, s32[40,1,6]{0,1,2:T(1,128)}, u32[]{:S(2)}) copy-start(s32[40,1,6]{0,1,2:T(1,128)} %param.20) | copy-start | bytes 2884
  6.5 22.0 %copy-start.14 = (s32[40,1,6]{0,1,2:T(1,128)S(1)}, s32[40,1,6]{0,1,2:T(1,128)}, u32[]{:S(2)}) copy-start(s32[40,1,6]{0,1,2:T(1,128)} %param.21) | copy-start | bytes 2884
  6.5 71.7 %copy-start.2 = (s32[8,1,8]{2,1,0:T(1,128)S(1)}, s32[8,1,8]{2,1,0:T(1,128)}, u32[]{:S(2)}) copy-start(s32[8,1,8]{2,1,0:T(1,128)} %param.22) | copy-start | bytes 772
  6.6 283.8 %all-gather.2.cloned.1.call-start = ((), (), s32[]{:S(2)}) async-start(), calls=%async_computation.4 | async-start | bytes 39321600 | tf_op jit(solution)/shard_map/all_gather | solution.py:84
  8.5 11.9 %all-to-all-start = ((s32[8,1,1]{2,1,0:T(1,128)}), s32[8,1,1]{2,1,0:T(1,128)S(1)}, u32[]{:S(2)}, u32[]{:S(2)}) async-start(s32[8,1,1]{2,1,0:T(1,128)} %reshape.365), calls=%async_computation | async-start | bytes 8192 | tf_op jit(solution)/shard_map/all_to_all | solution.py:66
  20.4 51.6 %all-to-all-start.3 = ((bf16[8,1,4,2,128,128]{5,4,3,2,1,0:T(8,128)(2,1)}), bf16[8,1,4,2,128,128]{5,4,3,2,1,0:T(8,128)(2,1)}, u32[]{:S(2)}, u32[]{:S(2)}) async-start(bf16[8,1,4,2,128,128]{5,4,3,2,1,0:T(8,128)(2,1)} %broadcast_select_fusion), calls=%async_computation.3 | async-start | bytes 4194304 | tf_op jit(solution)/shard_map/all_to_all | solution.py:45
  43.6 36.8 %copy-start.17 = (s32[8]{0:T(128)}, s32[8]{0:T(128)S(1)}, u32[]{:S(2)}) copy-start(s32[8]{0:T(128)S(1)} %subtract_reduce_fusion) | copy-start | bytes 100
  72.0 8.3 %all-to-all-start.1 = ((s32[8,1,4,2]{2,3,1,0:T(2,128)}), s32[8,1,4,2]{2,3,1,0:T(2,128)S(1)}, u32[]{:S(2)}, u32[]{:S(2)}) async-start(s32[8,1,4,2]{2,3,1,0:T(2,128)} %copy.222), calls=%async_computation.1 | async-start | bytes 16384 | tf_op jit(solution)/shard_map/all_to_all | solution.py:52
  78.0 55.1 %collective-permute-start.2 = (bf16[8,8,128,128]{3,2,1,0:T(8,128)(2,1)}, bf16[8,8,128,128]{3,2,1,0:T(8,128)(2,1)}, u32[]{:S(2)}, u32[]{:S(2)}) collective-permute-start(bf16[8,8,128,128]{3,2,1,0:T(8,128)(2,1)} %bitcast.22), channel_id=1, source_target_pairs={{0,6},{2,0},{4,2},{6,4},{1,7},{3,1},{5,3},{7,5},{8,14},{10,8},{12,... | collective-permute-start | bytes 6291464 | tf_op jit(solution)/shard_map/ppermute | solution.py:11
  80.3 47.5 %all-to-all-start.2 = ((s32[8,1,4,2]{2,3,1,0:T(2,128)}), s32[8,1,4,2]{2,3,1,0:T(2,128)S(1)}, u32[]{:S(2)}, u32[]{:S(2)}) async-start(s32[8,1,4,2]{2,3,1,0:T(2,128)} %copy.233), calls=%async_computation.2 | async-start | bytes 16384 | tf_op jit(solution)/shard_map/all_to_all | solution.py:59
  86.8 582.0 %all-reduce.2.cloned.1.call-start = ((), (), s32[]{:S(2)}) async-start(), calls=%async_computation.5 | async-start | bytes 4194304 | tf_op jit(solution)/shard_map/psum | solution.py:114
  87.0 43.9 %collective-permute-start = (s32[8,8]{0,1:T(8,128)S(1)}, s32[8,8]{0,1:T(8,128)S(1)}, u32[]{:S(2)}, u32[]{:S(2)}) collective-permute-start(s32[8,8]{0,1:T(8,128)S(1)} %bitcast.168), channel_id=1, source_target_pairs={{0,6},{2,0},{4,2},{6,4},{1,7},{3,1},{5,3},{7,5},{8,14},{10,8},{12,... | collective-permute-start | bytes 776 | tf_op jit(solution)/shard_map/ppermute | solution.py:11
  128.0 4.3 collective-permute-start.1
  132.4 5.5 collective-permute-start.3
  133.1 56.4 %collective-permute-start.5 = (bf16[8,8,128,128]{3,2,1,0:T(8,128)(2,1)}, bf16[8,8,128,128]{3,2,1,0:T(8,128)(2,1)}, u32[]{:S(2)}, u32[]{:S(2)}) collective-permute-start(bf16[8,8,128,128]{3,2,1,0:T(8,128)(2,1)} %collective-permute-done.2), channel_id=1, source_target_pairs={{0,6},{2,0},{4,2},{6,4},{1,7},{3,1},{5,3},{7,5},{8,14},{10,8},{12,... | collective-permute-start | bytes 6291464 | tf_op jit(solution)/shard_map/ppermute | solution.py:11
  134.7 46.9 %collective-permute-start.4 = (s32[8,8]{0,1:T(8,128)S(1)}, s32[8,8]{0,1:T(8,128)S(1)}, u32[]{:S(2)}, u32[]{:S(2)}) collective-permute-start(s32[8,8]{0,1:T(8,128)S(1)} %collective-permute-done.1), channel_id=1, source_target_pairs={{0,6},{2,0},{4,2},{6,4},{1,7},{3,1},{5,3},{7,5},{8,14},{10,8},{12,... | collective-permute-start | bytes 776 | tf_op jit(solution)/shard_map/ppermute | solution.py:11
  181.8 4.3 collective-permute-start.6
  183.4 4.3 collective-permute-start.7
  189.5 351.7 %collective-permute-start.8 = (bf16[8,8,128,128]{3,2,1,0:T(8,128)(2,1)}, bf16[8,8,128,128]{3,2,1,0:T(8,128)(2,1)S(1)}, u32[]{:S(2)}, u32[]{:S(2)}) collective-permute-start(bf16[8,8,128,128]{3,2,1,0:T(8,128)(2,1)} %collective-permute-done.5), channel_id=1, source_target_pairs={{0,6},{2,0},{4,2},{6,4},{1,7},{3,1},{5,3},{7,5},{8,14},{10,8},{12,... | collective-permute-start | bytes 6291464 | tf_op jit(solution)/shard_map/ppermute | solution.py:11
  554.1 24.9 %copy-start.3 = (s32[8,8,6]{1,2,0:T(8,128)S(1)}, s32[8,8,6]{1,2,0:T(8,128)}, u32[]{:S(2)}) copy-start(s32[8,8,6]{1,2,0:T(8,128)} %copy.227) | copy-start | bytes 4612
  554.1 24.9 %copy-start.7 = (s32[8,8]{1,0:T(8,128)S(1)}, s32[8,8]{1,0:T(8,128)}, u32[]{:S(2)}) copy-start(s32[8,8]{1,0:T(8,128)} %broadcast_select_fusion.1) | copy-start | bytes 772
  554.1 24.9 %copy-start.8 = (pred[8,8,6]{1,2,0:T(8,128)(4,1)S(1)}, pred[8,8,6]{1,2,0:T(8,128)(4,1)}, u32[]{:S(2)}) copy-start(pred[8,8,6]{1,2,0:T(8,128)(4,1)} %copy.236) | copy-start | bytes 1156
  579.0 15.7 %copy-start.4 = (s32[8,8,6]{1,2,0:T(8,128)S(1)}, s32[8,8,6]{1,2,0:T(8,128)}, u32[]{:S(2)}) copy-start(s32[8,8,6]{1,2,0:T(8,128)} %copy.243) | copy-start | bytes 4612
  579.0 15.7 %copy-start.9 = (pred[8,8,6]{1,2,0:T(8,128)(4,1)S(1)}, pred[8,8,6]{1,2,0:T(8,128)(4,1)}, u32[]{:S(2)}) copy-start(pred[8,8,6]{1,2,0:T(8,128)(4,1)} %copy.247) | copy-start | bytes 1156
  594.7 15.6 %copy-start.5 = (s32[8,8,6]{1,2,0:T(8,128)S(1)}, s32[8,8,6]{1,2,0:T(8,128)}, u32[]{:S(2)}) copy-start(s32[8,8,6]{1,2,0:T(8,128)} %copy.254) | copy-start | bytes 4612
  610.3 16.0 %copy-start.6 = (s32[8,8,6]{1,2,0:T(8,128)S(1)}, s32[8,8,6]{1,2,0:T(8,128)}, u32[]{:S(2)}) copy-start(s32[8,8,6]{1,2,0:T(8,128)} %copy.265) | copy-start | bytes 4612
  610.3 15.9 %copy-start.11 = (pred[8,8,6]{1,2,0:T(8,128)(4,1)S(1)}, pred[8,8,6]{1,2,0:T(8,128)(4,1)}, u32[]{:S(2)}) copy-start(pred[8,8,6]{1,2,0:T(8,128)(4,1)} %copy.269) | copy-start | bytes 1156
  626.2 19.4 %copy-start.12 = (s32[8,1,8]{2,1,0:T(1,128)S(1)}, s32[8,1,8]{2,1,0:T(1,128)}, u32[]{:S(2)}) copy-start(s32[8,1,8]{2,1,0:T(1,128)} %param.23) | copy-start | bytes 772
  626.2 19.7 %copy-start.18 = (s32[8]{0:T(128)S(1)}, s32[8]{0:T(128)}, u32[]{:S(2)}) copy-start(s32[8]{0:T(128)} %copy-done.17) | copy-start | bytes 100
  626.2 50.1 %copy-start.1 = (bf16[1,32,2,128,128]{4,3,2,1,0:T(8,128)(2,1)S(1)}, bf16[1,32,2,128,128]{4,3,2,1,0:T(8,128)(2,1)}, u32[]{:S(2)}) copy-start(bf16[1,32,2,128,128]{4,3,2,1,0:T(8,128)(2,1)} %param.15) | copy-start | bytes 6291460
  (2 other events, 23.2 us)
Sparse Core Ops, SparseCore 0:
  9.3 281.0 all-gather.1
  645.8 22.9 all-reduce.1
where the time goes:
time: 692 us; the launch traced here: 684 us
  local copies, waits for them, and re-layouts  259 us (37%)
  waiting for transfers between devices  238 us (34%)
  matrix products  120 us (17%)
  starting transfers between devices  28.9 us (4%)
  between operations  14.8 us (2%)
  blocking collectives  14.7 us (2%)
  other arithmetic  7.93 us (1%)
    gather x8, local copies, waits for them, and re-layouts, on_device(): selected_entries = jnp.take(layer_blocks, layer_row_index, axis=0)  135 us
    all_gather x1, waiting for transfers between devices, on_device(): lax.all_gather(b_blocks, 'row', axis=0, tiled=True)  101 us
    transpose x4, local copies, waits for them, and re-layouts, on_device(): jnp.einsum('rvab,rvsbe->rvsae', block_tiles, selected_entries, preferred_...  99.4 us
    dot_general x4, matrix products, on_device(): jnp.einsum('ruvs,rvsae->ruae', mapping, block_products, precision=lax.Pre...  66.5 us
    dot_general x4, matrix products, on_device(): jnp.einsum('rvab,rvsbe->rvsae', block_tiles, selected_entries, preferred_...  54 us
    ppermute x9, waiting for transfers between devices, shifted(): lax.ppermute(value, axis, [(i, (i + by) % length) for i in range(length)])  43.9 us
    all_to_all x1, waiting for transfers between devices, on_device(): lax.all_to_all(outgoing_live_flags.reshape((pair_count,) + lead_shape[2:]...  40.4 us
    all_to_all x1, waiting for transfers between devices, on_device(): lax.all_to_all(send_blocks.reshape((pair_count,) + lead_shape[2:] + (bloc...  28.4 us
  transfers between devices with their start and end apart: 15, of which 8 were waited for; matrix products, arithmetic and copies ran while one was open for 40% of the time, Pallas kernels for 0%

commit v1 on v0

v1 whole, which is shorter than its diff:
```python
import functools

import jax
import jax.numpy as jnp
from jax import lax
from jax.experimental import pallas as pl
from jax.experimental.pallas import tpu as pltpu
from jax.sharding import PartitionSpec as P

GW = 10
REACH = 16
MESH = pl.DeviceIdType.MESH


def stripe_kinds(total, stripe, panel):
    kinds = {}
    for rel in range(total // stripe):
        groups = []
        for g in range(stripe // GW):
            first = rel * stripe + g * GW
            if any((k + REACH) % total < panel + 2 * REACH for k in range(first, first + GW)):
                groups.append(g)
        if groups:
            kinds[rel] = (groups[0], groups[-1] + 1)
    return kinds


def kernel(
    n_row, n_col, n_depth, kinds, slots,
    pick_ref, source_ref, keep_ref, a_ref, b_ref, out_ref,
    abuf, bbuf, cbuf, pbuf, b_sem, a_send, a_recv, c_send, c_recv,
):
    row, col, depth = (lax.axis_index(name) for name in ("row", "col", "depth"))
    stripes = n_row * n_depth
    per_panel = stripes // n_col
    run = n_col * n_depth
    me = (row * n_col + col) * n_depth + depth
    my_stripe = row * n_depth + depth
    my_rel = lax.rem(my_stripe - per_panel * col + stripes, stripes)
    rels = sorted(kinds)
    blocks = b_ref.shape[0]
    share = pbuf.shape[2]
    targets = share * n_depth
    width = a_ref.shape[0] // stripes
    groups = width // slots
    active = functools.reduce(jnp.logical_or, [my_rel == rel for rel in rels])

    def a_part(ref, rel):
        low, high = kinds[rel]
        return ref.at[pl.ds(low * slots, (high - low) * slots)]

    b_copy = pltpu.make_async_copy(b_ref, bbuf.at[pl.ds(0, blocks)], b_sem)

    @pl.when(active)
    def _():
        b_copy.start()

    sends = []
    for c in range(n_col):
        for rel in rels:
            s = (per_panel * c + rel) % stripes
            low, high = kinds[rel]
            src = a_ref.at[pl.ds(s * width + low * slots, (high - low) * slots)]
            mine = (my_stripe == s) & (col == c)
            index = len(sends)
            remote = pltpu.make_async_remote_copy(
                src_ref=src,
                dst_ref=a_part(abuf.at[me], rel),
                send_sem=a_send.at[index],
                recv_sem=a_recv.at[me],
                device_id=(s // n_depth, c, s % n_depth),
                device_id_type=MESH,
            )
            local = pltpu.make_async_copy(src, a_part(abuf.at[me], rel), a_recv.at[me])
            sends.append((mine, remote))

            @pl.when(mine)
            def _(local=local):
                local.start()

            @pl.when(jnp.logical_not(mine))
            def _(remote=remote):
                remote.start()

    for rel in rels:
        low, high = kinds[rel]
        gaps = [g for g in range(groups) if not low <= g < high]
        if gaps:

            @pl.when(my_rel == rel)
            def _(gaps=gaps):
                def clear(p, carry):
                    for g in gaps:
                        for v in range(g * slots, (g + 1) * slots):
                            abuf[p, v] = jnp.zeros(abuf.shape[2:], abuf.dtype)
                    return carry

                lax.fori_loop(0, abuf.shape[0], clear, 0)

    def share_copy(target_row, d, rel):
        return pltpu.make_async_remote_copy(
            src_ref=cbuf.at[target_row, d],
            dst_ref=pbuf.at[rels.index(rel)],
            send_sem=c_send.at[target_row, d],
            recv_sem=c_recv.at[rels.index(rel)],
            device_id=(target_row, col, d),
            device_id_type=MESH,
        )

    @pl.when(active)
    def _():
        b_copy.wait()
        bbuf[blocks] = jnp.zeros(bbuf.shape[1:], bbuf.dtype)

        def one_run(t, carry):
            target_row = lax.rem(row + t, n_row)

            def one_row(q, inner):
                p = target_row * run + q
                for rel in rels:

                    @pl.when(my_rel == rel)
                    def _(rel=rel):
                        part = a_part(abuf.at[p], rel)
                        pltpu.make_async_copy(part, part, a_recv.at[p]).wait()

                base = p * (width * targets)
                for u in range(0, targets, 2):
                    total = None
                    for v in range(0, width, 2):
                        left = jnp.concatenate([abuf[p, v], abuf[p, v + 1]], axis=1)
                        right = jnp.concatenate(
                            [
                                jnp.concatenate(
                                    [
                                        bbuf[pick_ref[base + (v + i) * targets + u]],
                                        bbuf[pick_ref[base + (v + i) * targets + u + 1]],
                                    ],
                                    axis=1,
                                )
                                for i in range(2)
                            ],
                            axis=0,
                        )
                        term = jnp.dot(left, right, preferred_element_type=jnp.float32)
                        total = term if total is None else total + term
                    edge = abuf.shape[-1]
                    for i in range(2):
                        cbuf[target_row, (u + i) // share, q, (u + i) % share] = total[
                            :, i * edge : (i + 1) * edge
                        ].astype(cbuf.dtype)
                return inner

            lax.fori_loop(0, run, one_row, 0)
            for d in range(n_depth):
                own = (t == 0) & (depth == d)
                for rel in rels:

                    @pl.when((my_rel == rel) & jnp.logical_not(own))
                    def _(d=d, rel=rel):
                        share_copy(target_row, d, rel).start()

                    @pl.when((my_rel == rel) & own)
                    def _(d=d, rel=rel):
                        slot = rels.index(rel)
                        pltpu.make_async_copy(
                            cbuf.at[target_row, d], pbuf.at[slot], c_recv.at[slot]
                        ).start()

            return carry

        lax.fori_loop(0, n_row, one_run, 0)

    for slot in range(len(rels)):
        pltpu.make_async_copy(pbuf.at[slot], pbuf.at[slot], c_recv.at[slot]).wait()

    def finish(i, carry):
        q = source_ref[i]
        for u in range(share):
            value = pbuf[0, q, u].astype(jnp.float32)
            for slot in range(1, len(rels)):
                value = value + pbuf[slot, q, u].astype(jnp.float32)
            kept = keep_ref[i * share + u] > 0
            out_ref[i, u] = jnp.where(kept, value, jnp.float32(0.0)).astype(out_ref.dtype)
        return carry

    lax.fori_loop(0, run, finish, 0)

    for mine, remote in sends:

        @pl.when(jnp.logical_not(mine))
        def _(remote=remote):
            remote.wait_send()

    @pl.when(active)
    def _():
        def settle(t, carry):
            target_row = lax.rem(row + t, n_row)
            for d in range(n_depth):

                @pl.when(jnp.logical_not((t == 0) & (depth == d)))
                def _(d=d):
                    share_copy(target_row, d, rels[0]).wait_send()

            return carry

        lax.fori_loop(0, n_row, settle, 0)


def on_device(
    a_blocks, a_columns, a_live, atom_rows, b_blocks, b_columns, b_live, c_columns, c_live
):
    n_row, n_col, n_depth = (lax.axis_size(name) for name in ("row", "col", "depth"))
    row, col, depth = (lax.axis_index(name) for name in ("row", "col", "depth"))
    _, group_count, slots = a_columns.shape
    edge = a_blocks.shape[-1]
    stripe, _, list_width = b_columns.shape
    run, _, targets = c_columns.shape
    stripes = n_row * n_depth
    total = stripe * stripes
    share = targets // n_depth
    width = group_count * slots // stripes
    row_count = n_row * run
    kinds = stripe_kinds(total, stripe, total // n_col)
    my_stripe = row * n_depth + depth

    packed = jnp.concatenate(
        [
            jnp.where(a_live > 0, a_columns, -1).reshape(1, -1),
            c_columns.reshape(1, -1),
            jnp.broadcast_to(atom_rows.reshape(1, 1), (1, 128)),
        ],
        axis=1,
    )
    everyone = lax.all_gather(packed, ("row", "col", "depth"), axis=0, tiled=True)
    slot_count = group_count * slots
    a_keys = lax.dynamic_slice_in_dim(everyone[:, :slot_count], my_stripe * width, width, 1)
    panel_lists = everyone[:, slot_count : slot_count + run * targets].reshape(
        n_row, n_col, n_depth, run, targets
    )[:, :, 0]
    panel_lists = lax.dynamic_index_in_dim(panel_lists, col, 1, keepdims=False)
    atoms = everyone[:, slot_count + run * targets]
    hot = atoms[:, None] == jnp.arange(row_count, dtype=jnp.int32)
    wanted = jnp.sum(
        jnp.where(hot[:, :, None], panel_lists.reshape(1, row_count, targets), 0), axis=1
    )
    block_count = stripe * list_width
    b_keys = jnp.where(b_live > 0, b_columns, -1).reshape(-1)
    numbers = jnp.arange(block_count, dtype=jnp.int32)
    same_row = (a_keys - my_stripe * stripe)[:, :, None] == numbers // list_width
    same_column = wanted[:, :, None] == b_keys
    picks = block_count + jnp.sum(
        jnp.where(
            same_row[:, :, None, :] & same_column[:, None, :, :], numbers - block_count, 0
        ),
        axis=-1,
    )
    own_atoms = lax.dynamic_slice_in_dim(atoms, row * run, run, 0) - row * run
    places = jnp.arange(run, dtype=jnp.int32)
    source = jnp.sum(jnp.where(own_atoms[None, :] == places[:, None], places[None, :], 0), axis=1)
    keep = lax.dynamic_slice_in_dim(c_live[:, 0, :], depth * share, share, 1).reshape(-1)

    copies = n_col * len(kinds)
    result = pl.pallas_call(
        functools.partial(kernel, n_row, n_col, n_depth, kinds, slots),
        out_shape=jax.ShapeDtypeStruct((run, share, edge, edge), jnp.bfloat16),
        in_specs=[pl.BlockSpec(memory_space=pltpu.SMEM)] * 3
        + [pl.BlockSpec(memory_space=pl.ANY)] * 2,
        out_specs=pl.BlockSpec(memory_space=pltpu.VMEM),
        scratch_shapes=[
            pltpu.VMEM((row_count, width, edge, edge), jnp.bfloat16),
            pltpu.VMEM((block_count + 1, edge, edge), jnp.bfloat16),
            pltpu.VMEM((n_row, n_depth, run, share, edge, edge), jnp.bfloat16),
            pltpu.VMEM((len(kinds), run, share, edge, edge), jnp.bfloat16),
            pltpu.SemaphoreType.DMA,
            pltpu.SemaphoreType.DMA((copies,)),
            pltpu.SemaphoreType.DMA((row_count,)),
            pltpu.SemaphoreType.DMA((n_row, n_depth)),
            pltpu.SemaphoreType.DMA((len(kinds),)),
        ],
        compiler_params=pltpu.CompilerParams(
            has_side_effects=True, vmem_limit_bytes=60 * 1024 * 1024
        ),
    )(
        picks.reshape(-1),
        source,
        keep,
        a_blocks.reshape(-1, edge, edge),
        b_blocks.reshape(-1, edge, edge),
    )
    return result[:, None]


def solution(mesh):
    placed = (
        P(("row", "col", "depth"), None, None, None, None),
        P(("row", "col", "depth"), None, None),
        P(("row", "col", "depth"), None, None),
        P(("row", "col", "depth")),
        P(("row", "depth"), "col", None, None, None),
        P(("row", "depth"), "col", None),
        P(("row", "depth"), "col", None),
        P("row", "col", None),
        P("row", "col", None),
    )
    return jax.shard_map(
        on_device,
        mesh=mesh,
        in_specs=placed,
        out_specs=P("row", "col", "depth", None, None),
        check_vma=False,
    )
```

time: 692 us -> 244 us (0.35)
  local copies, waits for them, and re-layouts: 259 us -> 5.07 us
  waiting for transfers between devices: 238 us -> 0 us
  Pallas kernels: 0 us -> 190 us
  matrix products: 120 us -> 0 us
  starting transfers between devices: 28.9 us -> 0 us
  blocking collectives: 14.7 us -> 36.1 us
  between operations: 14.8 us -> 0.76 us
    pallas_call x0 -> x1, Pallas kernels: none -> 190 us  [on_device(): pl.pallas_call(functools.partial(kernel, n_row, n_col, n_depth, kinds, sl...]
    gather x23 -> x0, local copies, waits for them, and re-layouts: 146 us -> none  [the longest x8 135 us: on_device(): selected_entries = jnp.take(layer_blocks, layer_row_index, axis=0)]
    dot_general x8 -> x0, matrix products: 120 us -> none  [the longest x4 66.5 us: on_device(): jnp.einsum('ruvs,rvsae->ruae', mapping, block_products, precision=lax.Pre...]
    all_gather x1 -> x0, waiting for transfers between devices: 101 us -> none  [on_device(): lax.all_gather(b_blocks, 'row', axis=0, tiled=True)]
    transpose x4 -> x0, local copies, waits for them, and re-layouts: 99.4 us -> none  [on_device(): jnp.einsum('rvab,rvsbe->rvsae', block_tiles, selected_entries, preferred_...]
    all_to_all x4 -> x0, waiting for transfers between devices: 69.7 us -> none  [the longest x1 40.4 us: on_device(): lax.all_to_all(outgoing_live_flags.reshape((pair_count,) + lead_shape[2:]...]
    ppermute x9 -> x0, waiting for transfers between devices: 43.9 us -> none  [shifted(): lax.ppermute(value, axis, [(i, (i + by) % length) for i in range(length)])]
    all_to_all x4 -> x0, starting transfers between devices: 22.9 us -> none  [the longest x1 6.49 us: on_device(): lax.all_to_all(outgoing_live_flags.reshape((pair_count,) + lead_shape[2:]...]
  transfers between devices with their start and end apart: 15 -> 0, of which waited for: 8 -> 0; matrix products, arithmetic and copies ran while one was open for 40% -> 0% of each run, Pallas kernels for 0% -> 0%
where the time goes in v1:
time: 244 us; the launch traced here: 241 us
  Pallas kernels  190 us (78%)
  blocking collectives  36.1 us (15%)
  other arithmetic  8.99 us (4%)
  local copies, waits for them, and re-layouts  5.07 us (2%)
    pallas_call x1, Pallas kernels, on_device(): pl.pallas_call(functools.partial(kernel, n_row, n_col, n_depth, kinds, sl...  190 us
    all_gather x1, blocking collectives, on_device(): lax.all_gather(packed, ('row', 'col', 'depth'), axis=0, tiled=True)  36.1 us

profile of v1, /device:TPU:31, one launch (start us, length us, event | category | flops | bytes accessed | tf_op | source)
XLA Modules:
  0.0 241.4 jit_solution(15248861729723166228)
XLA Ops:
  0.0 0.0 copy-start
  0.7 0.7 compare_select_fusion.1
  1.4 0.7 compare_select_fusion
  2.1 0.5 broadcast.77
  2.6 1.3 reduce.11
  4.0 0.1 reshape.82
  4.1 0.0 copy-done
  4.1 0.1 dynamic-slice_reduce_fusion
  4.2 0.6 reshape.84.keep_ref
  4.7 0.1 copy.28
  4.8 0.1 reshape.81
  4.9 0.1 add_bitcast_fusion
  5.0 0.1 copy.30
  5.1 0.1 eq.73
  5.2 36.1 %all-gather = s32[32,1,256]{2,1,0:T(1,128)S(1)} all-gather(s32[1,1,256]{2,1,0:T(1,128)S(1)} %add_bitcast_fusion), channel_id=1, replica_groups=mesh['row'=4,'col'=4,'depth'=2] {'row','col','depth'}, dimensions={0}, use_global_device_ids=true | all-gather | bytes 33792 | tf_op jit(solution)/shard_map/all_gather | solution.py:235
  41.4 0.1 fusion
  41.5 0.1 subtract_reduce_fusion
  41.6 0.7 select_reduce_fusion.2.source_ref
  42.3 0.1 fusion.1
  42.4 0.1 dynamic-slice_subtract_fusion
  42.5 0.1 iota_compare_fusion
  42.5 0.1 reshape.83
  42.7 0.1 copy.32
  42.7 0.6 select_reduce_fusion.1
  43.4 0.1 broadcast_compare_fusion
  43.5 4.4 %select_reduce_fusion = s32[32,8,8]{2,1,0:T(8,128)S(1)} fusion(s32[240]{0:T(256)S(1)} %iota_add_fusion, pred[32,8,240]{2,1,0:T(8,128)(4,1)S(1)} %get-tuple-element.9, pred[32,8,240]{2,1,0:T(8,128)(4,1)S(1)} %get-tuple-element.10), kind=kLoop, calls=%fused_computation | loop fusion | flops 1472512 | bytes 132032 | tf_op jit(solution)/shard_map/reduce_sum | solution.py:252
  47.9 0.7 add.37.pick_ref
  48.6 190.4 %shard_map.91 = bf16[8,4,128,128]{3,2,1,0:T(8,128)(2,1)} custom-call(s32[2048]{0:T(1024)} %add.37.pick_ref, s32[8]{0:T(128)} %select_reduce_fusion.2.source_ref, s32[32]{0:T(128)} %reshape.84.keep_ref, bf16[64,128,128]{2,1,0:T(8,128)(2,1)} %bitcast.19, bf16[240,128,128]{2,1,0:T(8,128)(2,1)} %bitcast.17), custom_call_target="tpu_custom_call" | custom-call | tf_op jit(solution)/shard_map/pallas_call | solution.py:264
  239.1 2.3 copy.38
  (8 shorter events, 0.1 us)
Async XLA Ops:
  0.0 4.1 %copy-start = (s32[8,1,8]{2,1,0:T(1,128)S(1)}, s32[8,1,8]{2,1,0:T(1,128)}, u32[]{:S(2)}) copy-start(s32[8,1,8]{2,1,0:T(1,128)} %param.17) | copy-start | bytes 772

commit v2 on v1

v2 whole, which is shorter than its diff:
```python
import functools

import jax
import jax.numpy as jnp
from jax import lax
from jax.experimental import pallas as pl
from jax.experimental.pallas import tpu as pltpu
from jax.sharding import PartitionSpec as P

GW = 10
REACH = 16
MESH = pl.DeviceIdType.MESH


def stripe_kinds(total, stripe, panel):
    kinds = {}
    for rel in range(total // stripe):
        groups = []
        for g in range(stripe // GW):
            first = rel * stripe + g * GW
            if any((k + REACH) % total < panel + 2 * REACH for k in range(first, first + GW)):
                groups.append(g)
        if groups:
            kinds[rel] = (groups[0], groups[-1] + 1)
    return kinds


def kernel(
    n_row, n_col, n_depth, kinds, slots,
    pack_ref, keys_ref, keep_ref, a_ref, b_ref, out_ref,
    lbuf, picks, pick_s, abuf, bbuf, cbuf, mbuf, pbuf,
    l_send, l_recv, s_sem, b_sem, a_send, a_recv, m_send, m_recv, m_free, c_send, c_recv,
):
    row, col, depth = (lax.axis_index(name) for name in ("row", "col", "depth"))
    stripes = n_row * n_depth
    per_panel = stripes // n_col
    run = n_col * n_depth
    rows = n_row * run
    me = (row * n_col + col) * n_depth + depth
    my_stripe = row * n_depth + depth
    my_rel = lax.rem(my_stripe - per_panel * col + stripes, stripes)
    rels = sorted(kinds)
    blocks = b_ref.shape[0]
    share = pbuf.shape[2]
    targets = share * n_depth
    width = a_ref.shape[0] // stripes
    groups = width // slots
    active = functools.reduce(jnp.logical_or, [my_rel == rel for rel in rels])
    paired = [rel for rel in rels if rel ^ 1 in kinds and n_depth == 2]
    lone = [rel for rel in rels if rel not in paired]
    senders = sorted({rel // 2 * 2 if rel in paired else rel for rel in rels})

    def sender(rel):
        return senders.index(rel // 2 * 2 if rel in paired else rel)

    def a_part(ref, rel):
        low, high = kinds[rel]
        return ref.at[pl.ds(low * slots, (high - low) * slots)]

    def list_copy(offset):
        dest = lax.rem(me + offset, rows)
        dest_row, dest_col, dest_depth = dest // run, dest // n_depth % n_col, dest % n_depth
        return pltpu.make_async_remote_copy(
            src_ref=pack_ref.at[dest_row * n_depth + dest_depth],
            dst_ref=lbuf.at[me],
            send_sem=l_send,
            recv_sem=l_recv,
            device_id=(dest_row, dest_col, dest_depth),
            device_id_type=MESH,
        )

    pltpu.make_async_copy(pack_ref.at[my_stripe], lbuf.at[me], l_recv).start()

    def send_list(offset, carry):
        list_copy(offset).start()
        return carry

    lax.fori_loop(1, rows, send_list, 0)

    b_copy = pltpu.make_async_copy(b_ref, bbuf.at[pl.ds(0, blocks)], b_sem)

    @pl.when(active)
    def _():
        b_copy.start()

    sends = []
    for t in range(n_col):
        c = lax.rem(row + t, n_col)
        for rel in rels:
            s = lax.rem(per_panel * c + rel, stripes)
            low, high = kinds[rel]
            src = a_ref.at[pl.ds(s * width + low * slots, (high - low) * slots)]
            mine = (my_stripe == s) & (col == c)
            remote = pltpu.make_async_remote_copy(
                src_ref=src,
                dst_ref=a_part(abuf.at[me], rel),
                send_sem=a_send.at[len(sends)],
                recv_sem=a_recv.at[me],
                device_id=(s // n_depth, c, s % n_depth),
                device_id_type=MESH,
            )
            local = pltpu.make_async_copy(src, a_part(abuf.at[me], rel), a_recv.at[me])
            sends.append((mine, remote))

            @pl.when(mine)
            def _(local=local):
                local.start()

            @pl.when(jnp.logical_not(mine))
            def _(remote=remote):
                remote.start()

    for rel in rels:
        low, high = kinds[rel]
        gaps = [g for g in range(groups) if not low <= g < high]
        if gaps:

            @pl.when(my_rel == rel)
            def _(gaps=gaps):
                def clear(p, carry):
                    for g in gaps:
                        for v in range(g * slots, (g + 1) * slots):
                            abuf[p, v] = jnp.zeros(abuf.shape[2:], abuf.dtype)
                    return carry

                lax.fori_loop(0, rows, clear, 0)

    pltpu.make_async_copy(lbuf, lbuf, l_recv).wait()
    lanes = lbuf.shape[2]

    def match(p, carry):
        column_row = lbuf[p, 0:1, :]
        place = lbuf[p, 1:2, :]
        table = lbuf[(p // run * n_col + col) * n_depth, 8:, :]
        at = lax.broadcasted_iota(jnp.int32, (run, lanes), 0)
        wanted = jnp.sum(jnp.where(at == place, table, 0), axis=0, keepdims=True)
        hit = (keys_ref[1] == column_row) & (keys_ref[0] == wanted)
        number = lax.broadcasted_iota(jnp.int32, (blocks, lanes), 0)
        picks[pl.ds(p, 1), :] = jnp.min(
            jnp.where(hit, number, blocks), axis=0, keepdims=True
        )
        return carry

    lax.fori_loop(0, rows, match, 0)
    for q in range(run):
        picks[pl.ds(rows + q, 1), :] = lbuf[row * run + q, 1:2, :]
    to_scalars = pltpu.make_async_copy(picks, pick_s, s_sem)
    to_scalars.start()
    to_scalars.wait()

    def share_copy(target_row, d, slot):
        return pltpu.make_async_remote_copy(
            src_ref=cbuf.at[target_row, d],
            dst_ref=pbuf.at[slot],
            send_sem=c_send.at[target_row, d],
            recv_sem=c_recv.at[slot],
            device_id=(target_row, col, d),
            device_id_type=MESH,
        )

    def start_share(target_row, d, slot):
        own = (target_row == row) & (depth == d)

        @pl.when(jnp.logical_not(own))
        def _():
            share_copy(target_row, d, slot).start()

        @pl.when(own)
        def _():
            pltpu.make_async_copy(cbuf.at[target_row, d], pbuf.at[slot], c_recv.at[slot]).start()

    def settle_share(target_row, d):
        @pl.when(jnp.logical_not((target_row == row) & (depth == d)))
        def _():
            share_copy(target_row, d, 0).wait_send()

    is_paired = functools.reduce(jnp.logical_or, [my_rel == rel for rel in paired], False)

    def mate_copy(t, target_row):
        return pltpu.make_async_remote_copy(
            src_ref=cbuf.at[target_row, 1 - depth],
            dst_ref=mbuf.at[t % 2],
            send_sem=m_send.at[t % 2],
            recv_sem=m_recv.at[t % 2],
            device_id=(row, col, 1 - depth),
            device_id_type=MESH,
        )

    @pl.when(active)
    def _():
        b_copy.wait()
        bbuf[blocks] = jnp.zeros(bbuf.shape[1:], bbuf.dtype)

        def one_run(t, carry):
            target_row = lax.rem(col - t + n_row * n_col, n_row)

            def one_row(q, inner):
                p = target_row * run + q
                for rel in rels:

                    @pl.when(my_rel == rel)
                    def _(rel=rel):
                        part = a_part(abuf.at[p], rel)
                        pltpu.make_async_copy(part, part, a_recv.at[p]).wait()

                for u in range(0, targets, 2):
                    total = None
                    for v in range(0, width, 2):
                        left = jnp.concatenate([abuf[p, v], abuf[p, v + 1]], axis=1)
                        right = jnp.concatenate(
                            [
                                jnp.concatenate(
                                    [
                                        bbuf[pick_s[p, (v + i) * targets + u]],
                                        bbuf[pick_s[p, (v + i) * targets + u + 1]],
                                    ],
                                    axis=1,
                                )
                                for i in range(2)
                            ],
                            axis=0,
                        )
                        term = jnp.dot(left, right, preferred_element_type=jnp.float32)
                        total = term if total is None else total + term
                    edge = abuf.shape[-1]
                    for i in range(2):
                        cbuf[target_row, (u + i) // share, q, (u + i) % share] = total[
                            :, i * edge : (i + 1) * edge
                        ].astype(cbuf.dtype)
                return inner

            lax.fori_loop(0, run, one_row, 0)
            for rel in lone:

                @pl.when(my_rel == rel)
                def _(rel=rel):
                    for d in range(n_depth):
                        start_share(target_row, d, sender(rel))

            if paired:

                @pl.when(is_paired)
                def _():
                    @pl.when(t >= 2)
                    def _():
                        pl.semaphore_wait(m_free, 1)

                    exchange = mate_copy(t, target_row)
                    exchange.start()
                    exchange.wait()

                    def merge(q, inner):
                        for u in range(share):
                            cbuf[target_row, depth, q, u] = (
                                cbuf[target_row, depth, q, u].astype(jnp.float32)
                                + mbuf[t % 2, q, u].astype(jnp.float32)
                            ).astype(cbuf.dtype)
                        return inner

                    lax.fori_loop(0, run, merge, 0)

                    @pl.when(t < n_row - 2)
                    def _():
                        pl.semaphore_signal(
                            m_free,
                            inc=1,
                            device_id=(row, col, 1 - depth),
                            device_id_type=MESH,
                        )

                for slot, first in enumerate(senders):
                    if first in paired:

                        @pl.when(my_rel // 2 * 2 == first)
                        def _(slot=slot):
                            start_share(target_row, depth, slot)

            return carry

        lax.fori_loop(0, n_row, one_run, 0)

    for slot in range(len(senders)):
        pltpu.make_async_copy(pbuf.at[slot], pbuf.at[slot], c_recv.at[slot]).wait()

    def finish(i, carry):
        q = jnp.int32(0)
        for j in range(run):
            q = jnp.where(pick_s[rows + j, 0] == i, j, q)
        for u in range(share):
            value = pbuf[0, q, u].astype(jnp.float32)
            for slot in range(1, len(senders)):
                value = value + pbuf[slot, q, u].astype(jnp.float32)
            kept = keep_ref[i * share + u] > 0
            out_ref[i, u] = jnp.where(kept, value, jnp.float32(0.0)).astype(out_ref.dtype)
        return carry

    lax.fori_loop(0, run, finish, 0)

    sent = lbuf.at[pl.ds(0, rows - 1)]
    pltpu.make_async_copy(sent, sent, l_send).wait()
    for mine, remote in sends:

        @pl.when(jnp.logical_not(mine))
        def _(remote=remote):
            remote.wait_send()

    def settle(target_row, carry):
        for rel in lone:

            @pl.when(my_rel == rel)
            def _():
                for d in range(n_depth):
                    settle_share(target_row, d)

        if paired:

            @pl.when(is_paired)
            def _():
                settle_share(target_row, depth)

        return carry

    lax.fori_loop(0, n_row, settle, 0)


def on_device(
    a_blocks, a_columns, a_live, atom_rows, b_blocks, b_columns, b_live, c_columns, c_live
):
    n_row, n_col, n_depth = (lax.axis_size(name) for name in ("row", "col", "depth"))
    row, depth = (lax.axis_index(name) for name in ("row", "depth"))
    _, group_count, slots = a_columns.shape
    edge = a_blocks.shape[-1]
    stripe, _, list_width = b_columns.shape
    run, _, targets = c_columns.shape
    stripes = n_row * n_depth
    total = stripe * stripes
    share = targets // n_depth
    width = group_count * slots // stripes
    row_count = n_row * run
    kinds = stripe_kinds(total, stripe, total // n_col)
    senders = {rel // 2 * 2 if rel ^ 1 in kinds and n_depth == 2 else rel for rel in kinds}
    block_count = stripe * list_width
    lanes = -(-width * targets // 128) * 128
    spare = lanes - width * targets

    firsts = jnp.arange(stripes, dtype=jnp.int32)[:, None] * stripe
    a_keys = jnp.where(a_live > 0, a_columns, -total).reshape(stripes, width) - firsts
    a_keys = jnp.repeat(a_keys, targets, axis=1)
    a_keys = jnp.pad(a_keys, ((0, 0), (0, spare)), constant_values=-1)[:, None]
    place = jnp.broadcast_to((atom_rows - row * run).reshape(1, 1, 1), (stripes, 1, lanes))
    table = jnp.tile(c_columns[:, 0, :], (1, width))
    table = jnp.pad(table, ((0, 0), (0, spare)), constant_values=-2)
    pack = jnp.concatenate(
        [
            a_keys,
            place,
            jnp.zeros((stripes, 6, lanes), jnp.int32),
            jnp.broadcast_to(table[None], (stripes, run, lanes)),
        ],
        axis=1,
    )
    b_keys = jnp.where(b_live > 0, b_columns, -1).reshape(-1)
    b_rows = jnp.arange(block_count, dtype=jnp.int32) // list_width
    keys = jnp.broadcast_to(jnp.stack([b_keys, b_rows])[:, :, None], (2, block_count, lanes))
    keep = lax.dynamic_slice_in_dim(c_live[:, 0, :], depth * share, share, 1).reshape(-1)

    copies = n_col * len(kinds)
    result = pl.pallas_call(
        functools.partial(kernel, n_row, n_col, n_depth, kinds, slots),
        out_shape=jax.ShapeDtypeStruct((run, share, edge, edge), jnp.bfloat16),
        in_specs=[
            pl.BlockSpec(memory_space=pltpu.VMEM),
            pl.BlockSpec(memory_space=pltpu.VMEM),
            pl.BlockSpec(memory_space=pltpu.SMEM),
            pl.BlockSpec(memory_space=pl.ANY),
            pl.BlockSpec(memory_space=pl.ANY),
        ],
        out_specs=pl.BlockSpec(memory_space=pltpu.VMEM),
        scratch_shapes=[
            pltpu.VMEM((row_count, 8 + run, lanes), jnp.int32),
            pltpu.VMEM((row_count + run, lanes), jnp.int32),
            pltpu.SMEM((row_count + run, lanes), jnp.int32),
            pltpu.VMEM((row_count, width, edge, edge), jnp.bfloat16),
            pltpu.VMEM((block_count + 1, edge, edge), jnp.bfloat16),
            pltpu.VMEM((n_row, n_depth, run, share, edge, edge), jnp.bfloat16),
            pltpu.VMEM((2, run, share, edge, edge), jnp.bfloat16),
            pltpu.VMEM((len(senders), run, share, edge, edge), jnp.bfloat16),
            pltpu.SemaphoreType.DMA,
            pltpu.SemaphoreType.DMA,
            pltpu.SemaphoreType.DMA,
            pltpu.SemaphoreType.DMA,
            pltpu.SemaphoreType.DMA((copies,)),
            pltpu.SemaphoreType.DMA((row_count,)),
            pltpu.SemaphoreType.DMA((2,)),
            pltpu.SemaphoreType.DMA((2,)),
            pltpu.SemaphoreType.REGULAR,
            pltpu.SemaphoreType.DMA((n_row, n_depth)),
            pltpu.SemaphoreType.DMA((len(senders),)),
        ],
        compiler_params=pltpu.CompilerParams(
            has_side_effects=True, vmem_limit_bytes=60 * 1024 * 1024
        ),
    )(
        pack,
        keys,
        keep,
        a_blocks.reshape(-1, edge, edge),
        b_blocks.reshape(-1, edge, edge),
    )
    return result[:, None]


def solution(mesh):
    placed = (
        P(("row", "col", "depth"), None, None, None, None),
        P(("row", "col", "depth"), None, None),
        P(("row", "col", "depth"), None, None),
        P(("row", "col", "depth")),
        P(("row", "depth"), "col", None, None, None),
        P(("row", "depth"), "col", None),
        P(("row", "depth"), "col", None),
        P("row", "col", None),
        P("row", "col", None),
    )
    return jax.shard_map(
        on_device,
        mesh=mesh,
        in_specs=placed,
        out_specs=P("row", "col", "depth", None, None),
        check_vma=False,
    )
```

time: 244 us -> 173 us (0.71)
  the two profiles are of different devices: /device:TPU:31 before, /device:TPU:2 now
where the time goes in v2:
time: 173 us
  Pallas kernels  164 us (95%)
  local copies, waits for them, and re-layouts  5.24 us (3%)
  other arithmetic  2.2 us (1%)
    pallas_call x1, Pallas kernels, on_device(): pl.pallas_call(functools.partial(kernel, n_row, n_col, n_depth, kinds, sl...  164 us

profile of v2, /device:TPU:2, one launch (start us, length us, event | category | flops | bytes accessed | tf_op | source)
XLA Modules:
  0.0 172.6 jit_solution(11894970258858789437)
XLA Ops:
  0.0 0.0 copy-start
  0.7 0.1 pad.12.clone
  0.7 0.1 pad.13.clone
  0.8 0.7 compare_select_fusion.1
  1.5 0.7 compare_select_fusion
  2.2 0.0 copy-done
  2.2 0.1 dynamic-slice_reduce_fusion
  2.3 0.6 reshape.68.keep_ref
  2.9 0.1 copy.12
  3.0 0.1 reshape.66
  3.1 0.1 broadcast_subtract_fusion
  3.1 0.1 copy.13
  3.2 0.1 stack_reshape.3
  3.4 0.1 broadcast_in_dim.41
  3.4 0.1 reshape.67
  3.5 0.7 tile.11
  4.2 0.1 tile.12
  4.3 0.7 pad_add_fusion.pack_ref
  5.0 0.8 broadcast_in_dim.48.keys_ref
  5.8 164.4 %shard_map.91 = bf16[8,4,128,128]{3,2,1,0:T(8,128)(2,1)} custom-call(s32[8,16,128]{2,1,0:T(8,128)} %pad_add_fusion.pack_ref, s32[2,240,128]{2,1,0:T(8,128)} %broadcast_in_dim.48.keys_ref, s32[32]{0:T(128)} %reshape.68.keep_ref, bf16[64,128,128]{2,1,0:T(8,128)(2,1)} %bitcast.13, bf16[240,128,128]{2,1,0:T(8,128)(2,1)} %bitcast.11), custom_call_target="tpu_custom_call" | custom-call | tf_op jit(solution)/shard_map/pallas_call | solution.py:368
  170.3 2.3 %copy.17 = bf16[8,1,4,128,128]{4,3,2,1,0:T(8,128)(2,1)} copy(bf16[8,1,4,128,128]{4,3,2,1,0:T(8,128)(2,1)} %bitcast.12) | data formatting | bytes 2097152
  (7 shorter events, 0.0 us)
Async XLA Ops:
  0.0 2.2 %copy-start = (s32[8,1,8]{2,1,0:T(1,128)S(1)}, s32[8,1,8]{2,1,0:T(1,128)}, u32[]{:S(2)}) copy-start(s32[8,1,8]{2,1,0:T(1,128)} %param.17) | copy-start | bytes 772

commit v3 on v2

--- a/solution.py
+++ b/solution.py
@@ -25,10 +25,15 @@
     return kinds
 
 
+def flip(index, step, count):
+    return lax.rem(index // 2 + step // 2, count // 2) * 2 + lax.rem(index + step, 2)
+
+
 def kernel(
     n_row, n_col, n_depth, kinds, slots,
     pack_ref, keys_ref, keep_ref, a_ref, b_ref, out_ref,
     lbuf, picks, pick_s, abuf, bbuf, cbuf, mbuf, pbuf,
+    rbuf, r_recv, f_send,
     l_send, l_recv, s_sem, b_sem, a_send, a_recv, m_send, m_recv, m_free, c_send, c_recv,
 ):
     row, col, depth = (lax.axis_index(name) for name in ("row", "col", "depth"))
@@ -50,6 +55,8 @@
     lone = [rel for rel in rels if rel not in paired]
     senders = sorted({rel // 2 * 2 if rel in paired else rel for rel in rels})
 
+    relayed = (n_row, n_col, n_depth) == (4, 4, 2) and sorted(kinds) == [0, 1, 2, 7]
+
     def sender(rel):
         return senders.index(rel // 2 * 2 if rel in paired else rel)
 
@@ -84,12 +91,25 @@
         b_copy.start()
 
     sends = []
-    for t in range(n_col):
-        c = lax.rem(row + t, n_col)
+    for t in reversed(range(n_col)):
+        c = flip(row, t, n_col)
         for rel in rels:
             s = lax.rem(per_panel * c + rel, stripes)
             low, high = kinds[rel]
             src = a_ref.at[pl.ds(s * width + low * slots, (high - low) * slots)]
+            if relayed and t == 3 and rel == 1:
+                place = col * n_depth + depth
+                remote = pltpu.make_async_remote_copy(
+                    src_ref=src,
+                    dst_ref=rbuf.at[place],
+                    send_sem=a_send.at[len(sends)],
+                    recv_sem=r_recv.at[place],
+                    device_id=(flip(c, 1, n_row), c, 1 - lax.rem(c, 2)),
+                    device_id_type=MESH,
+                )
+                remote.start()
+                sends.append((False, remote))
+                continue
             mine = (my_stripe == s) & (col == c)
             remote = pltpu.make_async_remote_copy(
                 src_ref=src,
@@ -109,6 +129,30 @@
             @pl.when(jnp.logical_not(mine))
             def _(remote=remote):
                 remote.start()
+
+    forwards = (row == flip(col, 1, n_row)) & (depth == 1 - lax.rem(col, 2))
+
+    def forward_copy(q):
+        p = flip(col, 3, n_row) * run + q
+        return pltpu.make_async_remote_copy(
+            src_ref=rbuf.at[q],
+            dst_ref=abuf.at[p],
+            send_sem=f_send,
+            recv_sem=a_recv.at[p],
+            device_id=(col, col, 1),
+            device_id_type=MESH,
+        )
+
+    if relayed:
+
+        @pl.when(forwards)
+        def _():
+            def forward(q, carry):
+                pltpu.make_async_copy(rbuf.at[q], rbuf.at[q], r_recv.at[q]).wait()
+                forward_copy(q).start()
+                return carry
+
+            lax.fori_loop(0, run, forward, 0)
 
     for rel in rels:
         low, high = kinds[rel]
@@ -192,7 +236,7 @@
         bbuf[blocks] = jnp.zeros(bbuf.shape[1:], bbuf.dtype)
 
         def one_run(t, carry):
-            target_row = lax.rem(col - t + n_row * n_col, n_row)
+            target_row = flip(col, n_row - 1 - t, n_row)
 
             def one_row(q, inner):
                 p = target_row * run + q
@@ -298,7 +342,16 @@
 
     sent = lbuf.at[pl.ds(0, rows - 1)]
     pltpu.make_async_copy(sent, sent, l_send).wait()
+    if relayed:
+
+        @pl.when(forwards)
+        def _():
+            pltpu.make_async_copy(rbuf, rbuf, f_send).wait()
+
     for mine, remote in sends:
+        if mine is False:
+            remote.wait_send()
+            continue
 
         @pl.when(jnp.logical_not(mine))
         def _(remote=remote):
@@ -385,6 +438,9 @@
             pltpu.VMEM((n_row, n_depth, run, share, edge, edge), jnp.bfloat16),
             pltpu.VMEM((2, run, share, edge, edge), jnp.bfloat16),
             pltpu.VMEM((len(senders), run, share, edge, edge), jnp.bfloat16),
+            pltpu.VMEM((run if n_row == 4 else 1, width, edge, edge), jnp.bfloat16),
+            pltpu.SemaphoreType.DMA((run,)),
+            pltpu.SemaphoreType.DMA,
             pltpu.SemaphoreType.DMA,
             pltpu.SemaphoreType.DMA,
             pltpu.SemaphoreType.DMA,

time: 173 us -> 153 us (0.88)
  the two profiles are of different devices: /device:TPU:2 before, /device:TPU:31 now
where the time goes in v3:
time: 153 us; the launch traced here: 151 us
  Pallas kernels  143 us (93%)
  local copies, waits for them, and re-layouts  5.24 us (3%)
  other arithmetic  2.2 us (1%)
    pallas_call x1, Pallas kernels, on_device(): pl.pallas_call(functools.partial(kernel, n_row, n_col, n_depth, kinds, sl...  143 us

profile of v3, /device:TPU:31, one launch (start us, length us, event | category | flops | bytes accessed | tf_op | source)
XLA Modules:
  0.0 151.0 jit_solution(7340450468427939547)
XLA Ops:
  0.0 0.0 copy-start
  0.7 0.1 pad.12.clone
  0.7 0.1 pad.13.clone
  0.8 0.7 compare_select_fusion.1
  1.5 0.7 compare_select_fusion
  2.2 0.0 copy-done
  2.2 0.1 dynamic-slice_reduce_fusion
  2.3 0.6 reshape.68.keep_ref
  2.9 0.1 copy.12
  3.0 0.1 reshape.66
  3.1 0.1 broadcast_subtract_fusion
  3.1 0.1 copy.13
  3.2 0.1 stack_reshape.3
  3.4 0.1 broadcast_in_dim.41
  3.4 0.1 reshape.67
  3.5 0.7 tile.11
  4.2 0.1 tile.12
  4.3 0.7 pad_add_fusion.pack_ref
  5.0 0.8 broadcast_in_dim.48.keys_ref
  5.8 142.9 %shard_map.91 = bf16[8,4,128,128]{3,2,1,0:T(8,128)(2,1)} custom-call(s32[8,16,128]{2,1,0:T(8,128)} %pad_add_fusion.pack_ref, s32[2,240,128]{2,1,0:T(8,128)} %broadcast_in_dim.48.keys_ref, s32[32]{0:T(128)} %reshape.68.keep_ref, bf16[64,128,128]{2,1,0:T(8,128)(2,1)} %bitcast.13, bf16[240,128,128]{2,1,0:T(8,128)(2,1)} %bitcast.11), custom_call_target="tpu_custom_call" | custom-call | tf_op jit(solution)/shard_map/pallas_call | solution.py:421
  148.7 2.3 %copy.17 = bf16[8,1,4,128,128]{4,3,2,1,0:T(8,128)(2,1)} copy(bf16[8,1,4,128,128]{4,3,2,1,0:T(8,128)(2,1)} %bitcast.12) | data formatting | bytes 2097152
  (7 shorter events, 0.0 us)
Async XLA Ops:
  0.0 2.2 %copy-start = (s32[8,1,8]{2,1,0:T(1,128)S(1)}, s32[8,1,8]{2,1,0:T(1,128)}, u32[]{:S(2)}) copy-start(s32[8,1,8]{2,1,0:T(1,128)} %param.17) | copy-start | bytes 772

commit v4 on v3

--- a/solution.py
+++ b/solution.py
@@ -91,9 +91,9 @@
         b_copy.start()
 
     sends = []
-    for t in reversed(range(n_col)):
+    for heavy, t in [(h, t) for h in (True, False) for t in reversed(range(n_col))]:
         c = flip(row, t, n_col)
-        for rel in rels:
+        for rel in [r for r in rels if (r in (0, 1)) == heavy]:
             s = lax.rem(per_panel * c + rel, stripes)
             low, high = kinds[rel]
             src = a_ref.at[pl.ds(s * width + low * slots, (high - low) * slots)]

time: 153 us -> 159 us (1.039); the launches traced: 151 us -> 159 us
  Pallas kernels: 143 us -> 151 us
    pallas_call x1, Pallas kernels: 143 us -> 151 us  [on_device(): pl.pallas_call(functools.partial(kernel, n_row, n_col, n_depth, kinds, sl...]
where the time goes in v4:
time: 159 us
  Pallas kernels  151 us (95%)
  local copies, waits for them, and re-layouts  5.24 us (3%)
  other arithmetic  2.2 us (1%)
    pallas_call x1, Pallas kernels, on_device(): pl.pallas_call(functools.partial(kernel, n_row, n_col, n_depth, kinds, sl...  151 us

profile of v4, /device:TPU:31, one launch (start us, length us, event | category | flops | bytes accessed | tf_op | source)
XLA Modules:
  0.0 159.1 jit_solution(14143895705066481246)
XLA Ops:
  0.0 0.0 copy-start
  0.7 0.1 pad.12.clone
  0.7 0.1 pad.13.clone
  0.8 0.7 compare_select_fusion.1
  1.5 0.7 compare_select_fusion
  2.2 0.0 copy-done
  2.2 0.1 dynamic-slice_reduce_fusion
  2.3 0.6 reshape.68.keep_ref
  2.9 0.1 copy.12
  3.0 0.1 reshape.66
  3.1 0.1 broadcast_subtract_fusion
  3.1 0.1 copy.13
  3.2 0.1 stack_reshape.3
  3.4 0.1 broadcast_in_dim.41
  3.4 0.1 reshape.67
  3.5 0.7 tile.11
  4.2 0.1 tile.12
  4.3 0.7 pad_add_fusion.pack_ref
  5.0 0.8 broadcast_in_dim.48.keys_ref
  5.8 150.9 %shard_map.91 = bf16[8,4,128,128]{3,2,1,0:T(8,128)(2,1)} custom-call(s32[8,16,128]{2,1,0:T(8,128)} %pad_add_fusion.pack_ref, s32[2,240,128]{2,1,0:T(8,128)} %broadcast_in_dim.48.keys_ref, s32[32]{0:T(128)} %reshape.68.keep_ref, bf16[64,128,128]{2,1,0:T(8,128)(2,1)} %bitcast.13, bf16[240,128,128]{2,1,0:T(8,128)(2,1)} %bitcast.11), custom_call_target="tpu_custom_call" | custom-call | tf_op jit(solution)/shard_map/pallas_call | solution.py:421
  156.8 2.3 %copy.17 = bf16[8,1,4,128,128]{4,3,2,1,0:T(8,128)(2,1)} copy(bf16[8,1,4,128,128]{4,3,2,1,0:T(8,128)(2,1)} %bitcast.12) | data formatting | bytes 2097152
  (7 shorter events, 0.0 us)
Async XLA Ops:
  0.0 2.2 %copy-start = (s32[8,1,8]{2,1,0:T(1,128)S(1)}, s32[8,1,8]{2,1,0:T(1,128)}, u32[]{:S(2)}) copy-start(s32[8,1,8]{2,1,0:T(1,128)} %param.17) | copy-start | bytes 772
